TPU v7x, 256 devices: a whole 4x4x8 slice. The times are simulated.
256 devices in a mesh: seq: 64 (over z, x, y_lo), sub: 4 (over y_hi, core).
Axes of the slice: x: 4, y: 4 (y_hi: 2, y_lo: 2; y = y_hi * 2 + y_lo), z: 8, core: 2. Of those that a mesh axis runs over, the one named last changes fastest.
Arguments:
- features: bfloat16 [262144, 768], P(('seq', 'sub')), may hold values from -6 to 6
- kernel: bfloat16 [3, 768, 384], replicated, may hold values from -0.125 to 0.125
- offsets: float32 [384], replicated, may hold values from -3 to 3
- mixer: bfloat16 [384, 768], replicated, may hold values from -0.3125 to 0.3125
- biases: float32 [768], replicated, may hold values from -3 to 3
- cotangent: bfloat16 [262144, 768], P(('seq', 'sub')), may hold values from -6 to 6
Outputs:
- layer_output: bfloat16 [262144, 768], P(('seq', 'sub'))
- input_grad: bfloat16 [262144, 768], P(('seq', 'sub'))
- kernel_grad: float32 [3, 768, 384], replicated
- offset_grad: float32 [384], replicated
- mixer_grad: float32 [384, 768], replicated
- biases_grad: float32 [768], replicated
All inputs are finite; a program needn't handle non-finite values.
Results may differ from a plain program's by a relative error of at most 0.0075.
Values may be sent and summed in bfloat16 or wider, within the bound.
A program may use at most 64 MiB of HBM per device.

v0:
```python
import math
import jax
import jax.numpy as jnp
from jax import lax
from jax.sharding import PartitionSpec as P

DILATION_STEP = 8192


def from_behind(value, axis, steps):
    count = lax.axis_size(axis)
    pairs = [(source, (source + steps) % count) for source in range(count)]
    return lax.ppermute(value, axis, pairs)


def gelu_exact(values):
    return jax.nn.gelu(values, approximate=False)


def gelu_slope(values):
    normal_cdf = 0.5 * (1.0 + jax.scipy.special.erf(values / math.sqrt(2.0)))
    return normal_cdf + values * jnp.exp(-0.5 * values * values) / math.sqrt(2.0 * math.pi)


def contract_rows(left, right):
    return lax.dot_general(
        left, right, (((0,), (0,)), ((), ())), preferred_element_type=jnp.float32
    )


def times_transposed(left, right):
    return lax.dot_general(
        left, right, (((1,), (1,)), ((), ())), preferred_element_type=jnp.float32
    )


def local(features, kernel, offsets, mixer, biases, cotangent):
    partition_rows = features.shape[0]
    offset_distance = DILATION_STEP // (partition_rows * lax.axis_size("sub"))
    factor = 1.0 / math.sqrt(partition_rows * lax.axis_size("seq") * lax.axis_size("sub"))
    inputs = features.astype(jnp.float32)
    activated_output = gelu_exact(inputs).astype(jnp.bfloat16)
    send_early = jnp.dot(activated_output, kernel[0], preferred_element_type=jnp.float32).astype(
        jnp.bfloat16
    )
    send_late = jnp.dot(activated_output, kernel[2], preferred_element_type=jnp.float32).astype(
        jnp.bfloat16
    )
    tap_early = from_behind(send_early, "seq", offset_distance)
    tap_late = from_behind(send_late, "seq", -offset_distance)
    preact = (
        jnp.dot(activated_output, kernel[1], preferred_element_type=jnp.float32)
        + tap_early.astype(jnp.float32)
        + tap_late.astype(jnp.float32)
        + offsets
    )
    hidden = gelu_exact(preact).astype(jnp.bfloat16)
    layer_output = (
        inputs + jnp.dot(hidden, mixer, preferred_element_type=jnp.float32) + biases
    ).astype(jnp.bfloat16)
    cot_float = cotangent.astype(jnp.float32)
    mixer_part = contract_rows(hidden, cotangent) * factor
    biases_part = jnp.sum(cot_float, axis=0) * factor
    hidden_grad = times_transposed(cotangent, mixer)
    preactivation_grad = (hidden_grad * gelu_slope(preact)).astype(jnp.bfloat16)
    grad_later = from_behind(preactivation_grad, "seq", -offset_distance)
    grad_earlier = from_behind(preactivation_grad, "seq", offset_distance)
    kernel_part = (
        jnp.stack(
            [
                contract_rows(activated_output, grad_later),
                contract_rows(activated_output, preactivation_grad),
                contract_rows(activated_output, grad_earlier),
            ]
        )
        * factor
    )
    offset_part = jnp.sum(preactivation_grad.astype(jnp.float32), axis=0) * factor
    activated_output_grad = (
        times_transposed(preactivation_grad, kernel[1])
        + times_transposed(grad_later, kernel[0])
        + times_transposed(grad_earlier, kernel[2])
    )
    input_grad = (cot_float + activated_output_grad * gelu_slope(inputs)).astype(jnp.bfloat16)
    kernel_grad, offset_grad, mixer_grad, biases_grad = lax.psum(
        (kernel_part, offset_part, mixer_part, biases_part), ("seq", "sub")
    )
    return (layer_output, input_grad, kernel_grad, offset_grad, mixer_grad, biases_grad)


def solution(mesh):
    placed = (P(("seq", "sub"), None), P(), P(), P(), P(), P(("seq", "sub"), None))
    return jax.shard_map(
        local,
        mesh=mesh,
        in_specs=placed,
        out_specs=(P(("seq", "sub"), None), P(("seq", "sub"), None), P(), P(), P(), P()),
        check_vma=False,
    )
```

profile of v0, /device:TPU:2, one launch (start us, length us, event | category | flops | bytes accessed | tf_op | source)
XLA Modules:
  0.0 358.5 jit_solution(11011791587891050671)
XLA Ops:
  7.2 0.0 copy-start
  7.2 0.0 all-reduce.4.cloned.1.call-start
  7.2 0.0 copy-start.4
  7.2 8.0 %fusion.3 = bf16[1024,768]{1,0:T(8,128)(2,1)S(1)} fusion(bf16[1024,768]{1,0:T(8,128)(2,1)} %param.6), kind=kLoop, calls=%fused_computation.14 | loop fusion | flops 51904512 | bytes 3145728 | tf_op jit(solution)/shard_map/convert_element_type | solution.py:42
  15.3 0.0 copy-done.4
  15.3 1.0 convolution_convert_fusion.1
  16.3 0.0 copy-start.12
  16.3 1.6 collective-permute-start
  17.9 1.0 convolution_convert_fusion
  18.8 0.0 copy-start.1
  18.8 0.9 collective-permute-start.1
  19.7 15.9 %collective-permute-done = bf16[1024,384]{1,0:T(8,128)(2,1)S(1)} collective-permute-done((bf16[1024,384]{1,0:T(8,128)(2,1)S(1)}, bf16[1024,384]{1,0:T(8,128)(2,1)S(1)}, u32[]{:S(2)}, u32[]{:S(2)}) %collective-permute-start) | collective-permute-done | bytes 786464 | tf_op jit(solution)/shard_map/ppermute | solution.py:13
  35.6 2.3 collective-permute-done.1
  37.9 0.0 copy-done.12
  37.9 4.3 %fusion.43 = (bf16[1024,384]{1,0:T(8,128)(2,1)S(1)}, f32[1024,384]{1,0:T(8,128)S(1)}) fusion(f32[384]{0:T(512)S(1)} %copy-done.12, bf16[1024,384]{1,0:T(8,128)(2,1)S(1)} %collective-permute-done.1, bf16[1024,384]{1,0:T(8,128)(2,1)S(1)} %collective-permute-done, bf16[1024,768]{1,0:T(8,128)(2,1)S(1)} %fusion.3, bf16[3,768,384]{2,1,0:T(8,128)(2,1)S(1)} %copy-done.4), kind=kOutput, calls=%fused_computation.56 | convolution fusion | flops 631504896 | bytes 6096896 | tf_op jit(solution)/shard_map/dot_general | solution.py:52
  42.3 0.0 copy-done
  42.3 0.0 copy-done.1
  42.3 1.3 convert_reduce_fusion.1
  43.6 0.0 copy-start.6
  43.6 1.4 collective-permute-start.3
  45.0 3.9 %collective-permute-start.2 = (bf16[1024,384]{1,0:T(8,128)(2,1)S(1)}, bf16[1024,384]{1,0:T(8,128)(2,1)S(1)}, u32[]{:S(2)}, u32[]{:S(2)}) collective-permute-start(bf16[1024,384]{1,0:T(8,128)(2,1)S(1)} %get-tuple-element.13), channel_id=1, source_target_pairs={{0,248},{4,252},{8,0},{12,4},{16,8},{20,12},{24,16},{28,20},{32,24... | collective-permute-start | bytes 2359304 | tf_op jit(solution)/shard_map/ppermute | solution.py:13
  48.9 1.0 convolution_bitcast_fusion.1
  49.9 0.0 copy-done.6
  49.9 1.8 convolution_multiply_fusion
  51.7 13.6 %collective-permute-done.3 = bf16[1024,384]{1,0:T(8,128)(2,1)S(1)} collective-permute-done((bf16[1024,384]{1,0:T(8,128)(2,1)S(1)}, bf16[1024,384]{1,0:T(8,128)(2,1)S(1)}, u32[]{:S(2)}, u32[]{:S(2)}) %collective-permute-start.3) | collective-permute-done | bytes 786464 | tf_op jit(solution)/shard_map/ppermute | solution.py:13
  65.3 0.0 copy-start.9
  65.3 1.0 convolution_bitcast_fusion
  66.3 0.0 copy-done.9
  66.3 0.0 collective-permute-done.2
  66.3 0.0 copy-start.7
  66.3 0.9 copy-done.7
  67.2 1.0 convolution_bitcast_fusion.2
  68.2 2.0 maximum_multiply_fusion
  70.2 0.0 all-reduce.4.cloned.1.call-update
  70.3 0.3 convert_reduce_fusion
  70.6 80.6 %all-reduce = (f32[384]{0:T(512)}, f32[768]{0:T(1024)}) all-reduce(f32[384]{0:T(512)S(1)} %broadcast_multiply_fusion.1, f32[768]{0:T(1024)S(1)} %broadcast_multiply_fusion), channel_id=1, replica_groups=mesh['seq'=64,'sub'=4] {'seq','sub'}, use_global_device_ids=true, to_apply=%region_2.0 | all-reduce | flops 1152 | bytes 9216 | tf_op jit(solution)/shard_map/psum | solution.py:85
  151.2 0.0 copy-start.2
  151.2 0.0 copy-start.11
  151.2 2.4 fusion.62
  153.6 0.0 copy-done.2
  153.6 0.0 copy-done.11
  153.6 0.0 copy-start.5
  153.6 0.0 copy-start.8
  153.6 2.1 fusion.33
  155.8 0.0 copy-done.5
  155.8 0.0 copy-done.8
  155.8 0.0 copy-start.10
  155.8 1.0 fusion.59
  156.8 0.1 copy-done.10
  156.9 3.4 fusion
  160.4 186.1 %all-reduce.4.cloned.1.call-done = (f32[3,768,384]{2,1,0:T(8,128)}, f32[384,768]{1,0:T(8,128)}) async-done(((f32[3,768,384]{2,1,0:T(8,128)}, f32[384,768]{1,0:T(8,128)}), (f32[3,768,384]{2,1,0:T(8,128)}, f32[384,768]{1,0:T(8,128)})) %all-reduce.4.cloned.1.call-update) | async-done | bytes 4718608 | tf_op jit(solution)/shard_map/psum | solution.py:85
  346.5 0.0 copy-start.3
  346.5 4.1 %copy.14 = f32[3,768,384]{2,1,0:T(8,128)} copy(f32[3,768,384]{2,1,0:T(8,128)} %get-tuple-element.16) | data formatting | bytes 7077888
  350.6 0.0 copy-done.3
  350.6 1.0 copy.15
  (2 shorter events, 0.0 us)
Async XLA Ops:
  7.2 35.1 %copy-start = (bf16[384,768]{1,0:T(8,128)(2,1)S(1)}, bf16[384,768]{1,0:T(8,128)(2,1)}, u32[]{:S(2)}) copy-start(bf16[384,768]{1,0:T(8,128)(2,1)} %param.9) | copy-start | bytes 1769476
  7.2 339.3 %all-reduce.4.cloned.1.call-start = ((), (), s32[]{:S(2)}) async-start(), calls=%async_computation | async-start | bytes 9437184 | tf_op jit(solution)/shard_map/psum | solution.py:85
  7.2 8.1 %copy-start.4 = (bf16[3,768,384]{2,1,0:T(8,128)(2,1)S(1)}, bf16[3,768,384]{2,1,0:T(8,128)(2,1)}, u32[]{:S(2)}) copy-start(bf16[3,768,384]{2,1,0:T(8,128)(2,1)} %param.7) | copy-start | bytes 5308420
  16.3 21.7 %copy-start.12 = (f32[384]{0:T(512)S(1)}, f32[384]{0:T(512)}, u32[]{:S(2)}) copy-start(f32[384]{0:T(512)} %param.8) | copy-start | bytes 4612
  16.3 19.4 %collective-permute-start = (bf16[1024,384]{1,0:T(8,128)(2,1)S(1)}, bf16[1024,384]{1,0:T(8,128)(2,1)S(1)}, u32[]{:S(2)}, u32[]{:S(2)}) collective-permute-start(bf16[1024,384]{1,0:T(8,128)(2,1)S(1)} %convolution_convert_fusion.1), channel_id=1, source_target_pairs={{0,8},{4,12},{8,16},{12,20},{16,24},{20,28},{24,32},{28,36},{32,40... | collective-permute-start | bytes 2359304 | tf_op jit(solution)/shard_map/ppermute | solution.py:13
  18.8 23.4 %copy-start.1 = (bf16[1024,768]{1,0:T(8,128)(2,1)S(1)}, bf16[1024,768]{1,0:T(8,128)(2,1)}, u32[]{:S(2)}) copy-start(bf16[1024,768]{1,0:T(8,128)(2,1)} %param.11) | copy-start | bytes 4718596
  18.8 19.1 %collective-permute-start.1 = (bf16[1024,384]{1,0:T(8,128)(2,1)S(1)}, bf16[1024,384]{1,0:T(8,128)(2,1)S(1)}, u32[]{:S(2)}, u32[]{:S(2)}) collective-permute-start(bf16[1024,384]{1,0:T(8,128)(2,1)S(1)} %convolution_convert_fusion), channel_id=1, source_target_pairs={{0,248},{4,252},{8,0},{12,4},{16,8},{20,12},{24,16},{28,20},{32,24... | collective-permute-start | bytes 2359304 | tf_op jit(solution)/shard_map/ppermute | solution.py:13
  43.6 6.3 %copy-start.6 = (bf16[1024,384]{1,0:T(8,128)(2,1)}, bf16[1024,384]{1,0:T(8,128)(2,1)S(1)}, u32[]{:S(2)}) copy-start(bf16[1024,384]{1,0:T(8,128)(2,1)S(1)} %get-tuple-element.13) | copy-start | bytes 2359300
  43.6 21.6 %collective-permute-start.3 = (bf16[1024,384]{1,0:T(8,128)(2,1)S(1)}, bf16[1024,384]{1,0:T(8,128)(2,1)S(1)}, u32[]{:S(2)}, u32[]{:S(2)}) collective-permute-start(bf16[1024,384]{1,0:T(8,128)(2,1)S(1)} %get-tuple-element.13), channel_id=1, source_target_pairs={{0,8},{4,12},{8,16},{12,20},{16,24},{20,28},{24,32},{28,36},{32,40... | collective-permute-start | bytes 2359304 | tf_op jit(solution)/shard_map/ppermute | solution.py:13
  45.0 21.3 %collective-permute-start.2 = (bf16[1024,384]{1,0:T(8,128)(2,1)S(1)}, bf16[1024,384]{1,0:T(8,128)(2,1)S(1)}, u32[]{:S(2)}, u32[]{:S(2)}) collective-permute-start(bf16[1024,384]{1,0:T(8,128)(2,1)S(1)} %get-tuple-element.13), channel_id=1, source_target_pairs={{0,248},{4,252},{8,0},{12,4},{16,8},{20,12},{24,16},{28,20},{32,24... | collective-permute-start | bytes 2359304 | tf_op jit(solution)/shard_map/ppermute | solution.py:13
  65.3 1.0 copy-start.9
  66.3 0.9 copy-start.7
  151.2 2.4 copy-start.2
  151.2 2.4 copy-start.11
  153.6 2.1 copy-start.5
  153.6 2.1 copy-start.8
  155.8 1.1 copy-start.10
  346.5 4.1 %copy-start.3 = (f32[384,768]{1,0:T(8,128)S(1)}, f32[384,768]{1,0:T(8,128)}, u32[]{:S(2)}) copy-start(f32[384,768]{1,0:T(8,128)} %get-tuple-element.18) | copy-start | bytes 3538948
Sparse Core Ops, SparseCore 0:
  70.4 276.0 all-reduce.3
where the time goes:
time: 359 us; the launch traced here: 358 us
  waiting for transfers between devices  218 us (61%)
  blocking collectives  80.6 us (22%)
  matrix products  21.5 us (6%)
  between operations  14.2 us (4%)
  other arithmetic  10.4 us (3%)
  starting transfers between devices  7.73 us (2%)
  local copies, waits for them, and re-layouts  6.19 us (2%)
    psum x1, waiting for transfers between devices, local(): lax.psum((kernel_part, offset_part, mixer_part, biases_part), ('seq', 'su...  186 us
    psum x1, blocking collectives, local(): lax.psum((kernel_part, offset_part, mixer_part, biases_part), ('seq', 'su...  80.6 us
    ppermute x4, waiting for transfers between devices, from_behind(): return lax.ppermute(value, axis, pairs)  31.8 us
    dot_general x4, matrix products, times_transposed(): lax.dot_general(left, right, (((1,), (1,)), ((), ())), preferred_element_...  8.22 us
    convert_element_type x1, other arithmetic, local(): activated_output = gelu_exact(inputs).astype(jnp.bfloat16)  8.04 us
    ppermute x4, starting transfers between devices, from_behind(): return lax.ppermute(value, axis, pairs)  7.69 us
  transfers between devices with their start and end apart: 5, of which 4 were waited for; matrix products, arithmetic and copies ran while one was open for 4% of the time, Pallas kernels for 0%

commit v1 on v0

--- a/solution.py
+++ b/solution.py
@@ -83,7 +83,7 @@
     )
     input_grad = (cot_float + activated_output_grad * gelu_slope(inputs)).astype(jnp.bfloat16)
     kernel_grad, offset_grad, mixer_grad, biases_grad = lax.psum(
-        (kernel_part, offset_part, mixer_part, biases_part), ("seq", "sub")
+        lax.psum((kernel_part, offset_part, mixer_part, biases_part), "sub"), "seq"
     )
     return (layer_output, input_grad, kernel_grad, offset_grad, mixer_grad, biases_grad)
 

time: 359 us -> 819 us (2.28)
  waiting for transfers between devices: 218 us -> 593 us
  blocking collectives: 80.6 us -> 166 us
    psum x1 -> x2, waiting for transfers between devices: 186 us -> 562 us  [the longest x1 451 us: local(): lax.psum(lax.psum((kernel_part, offset_part, mixer_part, biases_part), 's...]
    psum x1 -> x2, blocking collectives: 80.6 us -> 166 us  [the longest x1 158 us: local(): lax.psum(lax.psum((kernel_part, offset_part, mixer_part, biases_part), 's...]
  transfers between devices with their start and end apart: 5 -> 6, of which waited for: 4 -> 5; matrix products, arithmetic and copies ran while one was open for 4% -> 2% of each run, Pallas kernels for 0% -> 0%
where the time goes in v1:
time: 819 us
  waiting for transfers between devices  593 us (72%)
  blocking collectives  166 us (20%)
  matrix products  21.5 us (3%)
  between operations  14.2 us (2%)
  other arithmetic  10.4 us (1%)
    psum x1, waiting for transfers between devices, local(): lax.psum(lax.psum((kernel_part, offset_part, mixer_part, biases_part), 's...  451 us
    psum x1, blocking collectives, local(): lax.psum(lax.psum((kernel_part, offset_part, mixer_part, biases_part), 's...  158 us
    psum x1, waiting for transfers between devices, local(): lax.psum((kernel_part, offset_part, mixer_part, biases_part), 'sub')  111 us
    ppermute x4, waiting for transfers between devices, from_behind(): return lax.ppermute(value, axis, pairs)  31.8 us
  transfers between devices with their start and end apart: 6, of which 5 were waited for; matrix products, arithmetic and copies ran while one was open for 2% of the time, Pallas kernels for 0%

profile of v1, /device:TPU:2, one launch (start us, length us, event | category | flops | bytes accessed | tf_op | source)
XLA Modules:
  0.0 819.1 jit_solution(146481156764189459)
XLA Ops:
  7.2 0.0 copy-start
  7.2 0.0 all-reduce.9.cloned.1.call-start
  7.2 0.0 copy-start.4
  7.2 8.0 fusion.3
  15.3 0.0 copy-done.4
  15.3 1.0 convolution_convert_fusion.1
  16.3 0.0 copy-start.12
  16.3 1.6 collective-permute-start
  17.9 1.0 convolution_convert_fusion
  18.8 0.0 copy-start.1
  18.8 0.9 collective-permute-start.1
  19.7 15.9 %collective-permute-done = bf16[1024,384]{1,0:T(8,128)(2,1)S(1)} collective-permute-done((bf16[1024,384]{1,0:T(8,128)(2,1)S(1)}, bf16[1024,384]{1,0:T(8,128)(2,1)S(1)}, u32[]{:S(2)}, u32[]{:S(2)}) %collective-permute-start) | collective-permute-done | bytes 786464 | tf_op jit(solution)/shard_map/ppermute | solution.py:13
  35.6 2.3 collective-permute-done.1
  37.9 0.0 copy-done.12
  37.9 4.3 fusion.43
  42.3 0.0 copy-done
  42.3 0.0 copy-done.1
  42.3 1.3 convert_reduce_fusion.1
  43.6 0.0 copy-start.6
  43.6 1.4 collective-permute-start.3
  45.0 3.9 collective-permute-start.2
  48.9 1.0 convolution_bitcast_fusion.1
  49.9 0.0 copy-done.6
  49.9 1.8 convolution_multiply_fusion
  51.7 13.6 %collective-permute-done.3 = bf16[1024,384]{1,0:T(8,128)(2,1)S(1)} collective-permute-done((bf16[1024,384]{1,0:T(8,128)(2,1)S(1)}, bf16[1024,384]{1,0:T(8,128)(2,1)S(1)}, u32[]{:S(2)}, u32[]{:S(2)}) %collective-permute-start.3) | collective-permute-done | bytes 786464 | tf_op jit(solution)/shard_map/ppermute | solution.py:13
  65.3 0.0 copy-start.9
  65.3 1.0 convolution_bitcast_fusion
  66.3 0.0 copy-done.9
  66.3 0.0 collective-permute-done.2
  66.3 0.0 copy-start.7
  66.3 0.9 copy-done.7
  67.2 1.0 convolution_bitcast_fusion.2
  68.2 2.0 maximum_multiply_fusion
  70.3 0.0 all-reduce.9.cloned.1.call-update
  70.3 0.0 all-reduce.7.cloned.1.call-start
  70.3 110.9 %all-reduce.9.cloned.1.call-done = (f32[3,768,384]{2,1,0:T(8,128)}, f32[384,768]{1,0:T(8,128)}) async-done(((f32[3,768,384]{2,1,0:T(8,128)}, f32[384,768]{1,0:T(8,128)}), (f32[3,768,384]{2,1,0:T(8,128)}, f32[384,768]{1,0:T(8,128)})) %all-reduce.9.cloned.1.call-update) | async-done | bytes 4718608 | tf_op jit(solution)/shard_map/psum | solution.py:86
  181.3 0.0 all-reduce.7.cloned.1.call-update
  181.3 0.3 convert_reduce_fusion
  181.6 7.6 all-reduce.2
  189.2 157.9 %all-reduce = (f32[384]{0:T(512)}, f32[768]{0:T(1024)}) all-reduce(f32[384]{0:T(512)S(1)} %get-tuple-element.10, f32[768]{0:T(1024)S(1)} %get-tuple-element.11), channel_id=1, replica_groups=mesh['seq'=64,'sub'=4] {'seq'}, use_global_device_ids=true, to_apply=%region_4.0 | all-reduce | flops 1152 | bytes 9216 | tf_op jit(solution)/shard_map/psum | solution.py:85
  347.1 0.0 copy-start.2
  347.1 0.0 copy-start.11
  347.1 2.4 fusion.62
  349.6 0.0 copy-done.2
  349.6 0.0 copy-done.11
  349.6 0.0 copy-start.5
  349.6 0.0 copy-start.8
  349.6 2.1 fusion.33
  351.7 0.0 copy-done.5
  351.7 0.0 copy-done.8
  351.7 0.0 copy-start.10
  351.7 1.0 fusion.59
  352.7 0.1 copy-done.10
  352.9 3.4 fusion
  356.3 450.8 %all-reduce.7.cloned.1.call-done = (f32[3,768,384]{2,1,0:T(8,128)}, f32[384,768]{1,0:T(8,128)}) async-done(((f32[3,768,384]{2,1,0:T(8,128)}, f32[384,768]{1,0:T(8,128)}), (f32[3,768,384]{2,1,0:T(8,128)}, f32[384,768]{1,0:T(8,128)})) %all-reduce.7.cloned.1.call-update) | async-done | bytes 4718608 | tf_op jit(solution)/shard_map/psum | solution.py:85
  807.1 0.0 copy-start.3
  807.1 4.1 copy.16
  811.2 0.0 copy-done.3
  811.2 1.0 copy.17
  (2 shorter events, 0.0 us)
Async XLA Ops:
  7.2 35.1 %copy-start = (bf16[384,768]{1,0:T(8,128)(2,1)S(1)}, bf16[384,768]{1,0:T(8,128)(2,1)}, u32[]{:S(2)}) copy-start(bf16[384,768]{1,0:T(8,128)(2,1)} %param.9) | copy-start | bytes 1769476
  7.2 174.1 %all-reduce.9.cloned.1.call-start = ((), (), s32[]{:S(2)}) async-start(), calls=%async_computation.1 | async-start | bytes 9437184 | tf_op jit(solution)/shard_map/psum | solution.py:86
  7.2 8.1 copy-start.4
  16.3 21.7 %copy-start.12 = (f32[384]{0:T(512)S(1)}, f32[384]{0:T(512)}, u32[]{:S(2)}) copy-start(f32[384]{0:T(512)} %param.8) | copy-start | bytes 4612
  16.3 19.4 %collective-permute-start = (bf16[1024,384]{1,0:T(8,128)(2,1)S(1)}, bf16[1024,384]{1,0:T(8,128)(2,1)S(1)}, u32[]{:S(2)}, u32[]{:S(2)}) collective-permute-start(bf16[1024,384]{1,0:T(8,128)(2,1)S(1)} %convolution_convert_fusion.1), channel_id=1, source_target_pairs={{0,8},{4,12},{8,16},{12,20},{16,24},{20,28},{24,32},{28,36},{32,40... | collective-permute-start | bytes 2359304 | tf_op jit(solution)/shard_map/ppermute | solution.py:13
  18.8 23.4 %copy-start.1 = (bf16[1024,768]{1,0:T(8,128)(2,1)S(1)}, bf16[1024,768]{1,0:T(8,128)(2,1)}, u32[]{:S(2)}) copy-start(bf16[1024,768]{1,0:T(8,128)(2,1)} %param.11) | copy-start | bytes 4718596
  18.8 19.1 %collective-permute-start.1 = (bf16[1024,384]{1,0:T(8,128)(2,1)S(1)}, bf16[1024,384]{1,0:T(8,128)(2,1)S(1)}, u32[]{:S(2)}, u32[]{:S(2)}) collective-permute-start(bf16[1024,384]{1,0:T(8,128)(2,1)S(1)} %convolution_convert_fusion), channel_id=1, source_target_pairs={{0,248},{4,252},{8,0},{12,4},{16,8},{20,12},{24,16},{28,20},{32,24... | collective-permute-start | bytes 2359304 | tf_op jit(solution)/shard_map/ppermute | solution.py:13
  43.6 6.3 copy-start.6
  43.6 21.6 %collective-permute-start.3 = (bf16[1024,384]{1,0:T(8,128)(2,1)S(1)}, bf16[1024,384]{1,0:T(8,128)(2,1)S(1)}, u32[]{:S(2)}, u32[]{:S(2)}) collective-permute-start(bf16[1024,384]{1,0:T(8,128)(2,1)S(1)} %get-tuple-element.17), channel_id=1, source_target_pairs={{0,8},{4,12},{8,16},{12,20},{16,24},{20,28},{24,32},{28,36},{32,40... | collective-permute-start | bytes 2359304 | tf_op jit(solution)/shard_map/ppermute | solution.py:13
  45.0 21.3 %collective-permute-start.2 = (bf16[1024,384]{1,0:T(8,128)(2,1)S(1)}, bf16[1024,384]{1,0:T(8,128)(2,1)S(1)}, u32[]{:S(2)}, u32[]{:S(2)}) collective-permute-start(bf16[1024,384]{1,0:T(8,128)(2,1)S(1)} %get-tuple-element.17), channel_id=1, source_target_pairs={{0,248},{4,252},{8,0},{12,4},{16,8},{20,12},{24,16},{28,20},{32,24... | collective-permute-start | bytes 2359304 | tf_op jit(solution)/shard_map/ppermute | solution.py:13
  65.3 1.0 copy-start.9
  66.3 0.9 copy-start.7
  70.3 736.8 %all-reduce.7.cloned.1.call-start = ((), (), s32[]{:S(2)}) async-start(), calls=%async_computation | async-start | bytes 9437184 | tf_op jit(solution)/shard_map/psum | solution.py:85
  347.1 2.4 copy-start.2
  347.1 2.4 copy-start.11
  349.6 2.1 copy-start.5
  349.6 2.1 copy-start.8
  351.7 1.1 copy-start.10
  807.1 4.1 copy-start.3
Sparse Core Ops, SparseCore 0:
  70.4 110.8 all-reduce.8
  184.0 623.0 all-reduce.6
